TPU v7x, 512 devices: a whole 4x8x8 slice. The times are simulated.
512 devices in a mesh: row: 16 (over y, core), col: 32 (over x, z).
Axes of the slice: x: 4, y: 8, z: 8, core: 2. Of those that a mesh axis runs over, the one named last changes fastest.
Arguments:
- rhs: bfloat16 [4, 16, 32, 64, 256], P(None, 'row', 'col'), may hold values from -6 to 6
- dinv: float32 [4, 16, 32, 64, 64], P(None, 'row', 'col'), may hold values from -1.5 to 1.5, as said below
- lower: bfloat16 [6, 16, 32, 32, 64, 128], P(None, 'row', 'col'), may hold values from -0.0625 to 0.0625
- sources: int32 [6, 16, 32, 32, 2], P(None, 'row', 'col'), may hold values from -1 to 15, as said below
Outputs:
- solution: float32 [4, 16, 32, 64, 256], P(None, 'row', 'col')
Inputs may be any that keep to these rules, and one draw needn't show every extreme that they name: `dinv`: lower triangular. `sources`: for each level pair, holder and target, the live entries are distinct; in every level pair every device has a target with all 2 entries live.
All inputs are finite; a program needn't handle non-finite values.
Results may differ from a plain program's by a relative error of at most 0.002.
Values may be sent and summed in bfloat16 or wider, within the bound.
No kernel may reach another device: no remote copies, remote signals or barrier semaphores. Data moves between devices by JAX's collectives and lax.ppermute only.
A program may use at most 64 MiB of HBM per device.

v0:
```python
import jax
import jax.numpy as jnp
from jax import lax
from jax.sharding import PartitionSpec as P


def level_terms(blocks, indices, gathered):
    clipped = jnp.maximum(indices, 0)
    picked = jnp.take(gathered, clipped, axis=0)
    picked = jnp.where((indices >= 0)[:, :, None, None], picked, jnp.zeros((), gathered.dtype))
    peer_count, per_count, block_rows, rhs_width = picked.shape
    picked = picked.reshape(peer_count, per_count * block_rows, rhs_width)
    return jnp.einsum("qik,qkn->qin", blocks, picked, preferred_element_type=jnp.float32)


def on_device(rhs, dinv, lower, sources):
    levels = rhs.shape[0]
    pair_of = {}
    for section in range(levels):
        for target in range(section + 1, levels):
            pair_of[section, target] = len(pair_of)
    gathered = []
    results = []
    for section in range(levels):
        residual = rhs[section, 0, 0].astype(jnp.float32)
        if section:
            partial = None
            for earlier in range(section):
                pair = pair_of[earlier, section]
                term = level_terms(lower[pair, 0, 0], sources[pair, 0, 0], gathered[earlier])
                partial = term if partial is None else partial + term
            arrived = lax.all_to_all(
                partial.astype(jnp.bfloat16), "col", split_axis=0, concat_axis=0, tiled=True
            )
            residual = residual - jnp.sum(arrived.astype(jnp.float32), axis=0)
        solution = jnp.dot(
            dinv[section, 0, 0],
            residual,
            precision=lax.Precision.HIGHEST,
            preferred_element_type=jnp.float32,
        )
        results.append(solution)
        if section + 1 < levels:
            solved = solution.astype(jnp.bfloat16)
            gathered.append(lax.all_gather(solved[None], "row", axis=0, tiled=True))
    return jnp.stack(results)[:, None, None]


def solution(mesh):
    in_specs = (
        P(None, "row", "col", None, None),
        P(None, "row", "col", None, None),
        P(None, "row", "col", None, None, None),
        P(None, "row", "col", None, None),
    )
    out_specs = P(None, "row", "col", None, None)
    return jax.shard_map(
        on_device, mesh=mesh, in_specs=in_specs, out_specs=out_specs, check_vma=False
    )
```

profile of v0, /device:TPU:8, one launch (start us, length us, event | category | flops | bytes accessed | tf_op | source)
XLA Modules:
  0.0 183.5 jit_solution(16684669490472690284)
XLA Ops:
  0.0 1.3 compare_and_fusion.1
  1.3 1.4 compare_bitcast_fusion.1
  2.7 0.1 copy.26
  2.8 0.1 reshape.152
  2.9 0.9 fusion.40
  3.8 21.4 %all-gather = bf16[1024,256]{1,0:T(8,128)(2,1)S(1)} all-gather(bf16[64,256]{1,0:T(8,128)(2,1)S(1)} %get-tuple-element.34), channel_id=2, replica_groups=mesh['row'=16,'col'=32] {'row'}, dimensions={0}, use_global_device_ids=true | all-gather | bytes 557056 | tf_op jit(solution)/shard_map/all_gather | solution.py:45
  25.2 0.1 copy.25
  25.3 0.1 copy.24
  25.4 0.7 gather_fusion
  26.1 0.3 select_select_fusion.5
  26.5 2.5 %fusion = bf16[32,64,256]{2,1,0:T(8,128)(2,1)} fusion(bf16[32,128,256]{2,1,0:T(8,128)(2,1)S(1)} %bitcast.153, bf16[6,1,1,32,64,128]{5,4,3,2,1,0:T(8,128)(2,1)} %param.8), kind=kOutput, calls=%fused_computation.18 | convolution fusion | flops 134742016 | bytes 3670016 | tf_op jit(solution)/shard_map/qik,qkn->qin/dot_general | solution.py:13
  28.9 9.5 %all-to-all-start = ((bf16[32,64,256]{2,1,0:T(8,128)(2,1)}), bf16[32,64,256]{2,1,0:T(8,128)(2,1)}, u32[]{:S(2)}, u32[]{:S(2)}) async-start(bf16[32,64,256]{2,1,0:T(8,128)(2,1)} %fusion), calls=%async_computation | async-start | bytes 2097152 | tf_op jit(solution)/shard_map/all_to_all | solution.py:32
  38.5 0.1 copy.32
  38.5 0.1 reshape.160
  38.7 0.1 copy.31
  38.8 0.1 copy.30
  38.9 0.1 copy.29
  38.9 0.1 reshape.156
  39.1 0.7 gather_fusion.1
  39.8 0.1 copy.28
  39.9 0.1 copy.27
  40.0 0.3 select_select_fusion.4
  40.3 2.9 %fusion.9 = f32[32,256,64]{1,2,0:T(8,128)} fusion(bf16[32,128,256]{2,1,0:T(8,128)(2,1)S(1)} %bitcast.159, bf16[6,1,1,32,64,128]{5,4,3,2,1,0:T(8,128)(2,1)} %param.8), kind=kOutput, calls=%fused_computation.28 | convolution fusion | flops 134217728 | bytes 4718592 | tf_op jit(solution)/shard_map/qik,qkn->qin/dot_general | solution.py:13
  43.2 24.3 %all-to-all-done = bf16[32,64,256]{2,1,0:T(8,128)(2,1)} async-done(((bf16[32,64,256]{2,1,0:T(8,128)(2,1)}), bf16[32,64,256]{2,1,0:T(8,128)(2,1)}, u32[]{:S(2)}, u32[]{:S(2)}) %all-to-all-start) | async-done | bytes 1048608 | tf_op jit(solution)/shard_map/all_to_all | solution.py:32
  67.5 1.4 convert_reduce_fusion.2
  68.9 0.2 bitcast_convert_fusion.1
  69.2 17.4 %all-gather.1 = bf16[1024,256]{1,0:T(8,128)(2,1)S(1)} all-gather(bf16[64,256]{1,0:T(8,128)(2,1)S(1)} %get-tuple-element.36), channel_id=3, replica_groups=mesh['row'=16,'col'=32] {'row'}, dimensions={0}, use_global_device_ids=true | all-gather | bytes 557056 | tf_op jit(solution)/shard_map/all_gather | solution.py:45
  86.6 0.7 gather_fusion.2
  87.3 0.3 select_select_fusion.3
  87.6 1.2 copy-done.2
  88.9 2.6 %fusion.1 = bf16[32,64,256]{2,1,0:T(8,128)(2,1)} fusion(f32[32,256,64]{1,2,0:T(8,128)S(1)} %copy-done.2, bf16[32,128,256]{2,1,0:T(8,128)(2,1)S(1)} %bitcast.164, bf16[6,1,1,32,64,128]{5,4,3,2,1,0:T(8,128)(2,1)} %param.8), kind=kOutput, calls=%fused_computation.19 | convolution fusion | flops 135266304 | bytes 5767168 | tf_op jit(solution)/shard_map/qik,qkn->qin/dot_general | solution.py:13
  91.5 5.2 %all-to-all-start.1 = ((bf16[32,64,256]{2,1,0:T(8,128)(2,1)}), bf16[32,64,256]{2,1,0:T(8,128)(2,1)}, u32[]{:S(2)}, u32[]{:S(2)}) async-start(bf16[32,64,256]{2,1,0:T(8,128)(2,1)} %fusion.1), calls=%async_computation.1 | async-start | bytes 2097152 | tf_op jit(solution)/shard_map/all_to_all | solution.py:32
  96.8 0.1 copy.41
  96.8 0.7 reshape.172
  97.5 0.1 copy.40
  97.6 0.1 copy.39
  97.8 0.1 copy.38
  97.8 0.6 reshape.168
  98.5 0.1 copy.37
  98.6 0.7 copy.36
  99.4 0.1 reshape.164
  99.5 0.7 gather_fusion.3
  100.2 0.7 copy.34
  100.9 0.8 copy.33
  101.6 0.7 pad_clamp_fusion
  102.3 0.6 pad_clamp_fusion.1
  102.9 0.3 select_select_fusion.2
  103.3 2.8 %fusion.6 = f32[32,256,64]{1,2,0:T(8,128)} fusion(bf16[32,128,256]{2,1,0:T(8,128)(2,1)S(1)} %bitcast.161, bf16[6,1,1,32,64,128]{5,4,3,2,1,0:T(8,128)(2,1)} %param.8), kind=kOutput, calls=%fused_computation.25 | convolution fusion | flops 134217728 | bytes 4718592 | tf_op jit(solution)/shard_map/qik,qkn->qin/dot_general | solution.py:13
  106.1 0.7 gather_fusion.4
  106.8 0.3 select_select_fusion.1
  107.1 2.8 %fusion.4 = f32[32,256,64]{1,2,0:T(8,128)} fusion(bf16[32,128,256]{2,1,0:T(8,128)(2,1)S(1)} %bitcast.162, bf16[6,1,1,32,64,128]{5,4,3,2,1,0:T(8,128)(2,1)} %param.8), kind=kOutput, calls=%fused_computation.23 | convolution fusion | flops 134217728 | bytes 4718592 | tf_op jit(solution)/shard_map/qik,qkn->qin/dot_general | solution.py:13
  110.0 15.9 %all-to-all-done.1 = bf16[32,64,256]{2,1,0:T(8,128)(2,1)} async-done(((bf16[32,64,256]{2,1,0:T(8,128)(2,1)}), bf16[32,64,256]{2,1,0:T(8,128)(2,1)}, u32[]{:S(2)}, u32[]{:S(2)}) %all-to-all-start.1) | async-done | bytes 1048608 | tf_op jit(solution)/shard_map/all_to_all | solution.py:32
  125.8 1.4 convert_reduce_fusion.1
  127.2 0.2 bitcast_convert_fusion
  127.4 16.4 %all-gather.2 = bf16[1024,256]{1,0:T(8,128)(2,1)S(1)} all-gather(bf16[64,256]{1,0:T(8,128)(2,1)S(1)} %get-tuple-element.38), channel_id=4, replica_groups=mesh['row'=16,'col'=32] {'row'}, dimensions={0}, use_global_device_ids=true | all-gather | bytes 557056 | tf_op jit(solution)/shard_map/all_gather | solution.py:45
  143.8 0.7 gather_fusion.5
  144.5 0.3 select_select_fusion
  144.8 1.2 copy-done
  146.1 0.6 copy-done.1
  146.7 1.7 fusion.2
  148.4 34.0 %all_to_all.15 = bf16[32,64,256]{2,1,0:T(8,128)(2,1)S(1)} all-to-all(bf16[32,64,256]{2,1,0:T(8,128)(2,1)S(1)} %fusion.2), channel_id=1, replica_groups=mesh['row'=16,'col'=32] {'col'}, dimensions={0} | all-to-all | bytes 2097152 | tf_op jit(solution)/shard_map/all_to_all | solution.py:32
  182.4 0.2 convert_reduce_fusion
  182.6 0.2 convolution_bitcast_fusion
  182.8 0.7 maximum_bitcast_fusion
  (26 shorter events, 0.2 us)
Async XLA Ops:
  28.9 38.6 %all-to-all-start = ((bf16[32,64,256]{2,1,0:T(8,128)(2,1)}), bf16[32,64,256]{2,1,0:T(8,128)(2,1)}, u32[]{:S(2)}, u32[]{:S(2)}) async-start(bf16[32,64,256]{2,1,0:T(8,128)(2,1)} %fusion), calls=%async_computation | async-start | bytes 2097152 | tf_op jit(solution)/shard_map/all_to_all | solution.py:32
  40.3 28.6 %copy-start.3 = (f32[4,1,1,64,64]{4,3,2,1,0:T(8,128)S(1)}, f32[4,1,1,64,64]{4,3,2,1,0:T(8,128)}, u32[]{:S(2)}) copy-start(f32[4,1,1,64,64]{4,3,2,1,0:T(8,128)} %param.7) | copy-start | bytes 196612
  40.3 28.6 %copy-start.4 = (bf16[4,1,1,64,256]{4,3,2,1,0:T(8,128)(2,1)S(1)}, bf16[4,1,1,64,256]{4,3,2,1,0:T(8,128)(2,1)}, u32[]{:S(2)}) copy-start(bf16[4,1,1,64,256]{4,3,2,1,0:T(8,128)(2,1)} %param.6) | copy-start | bytes 393220
  87.3 1.6 copy-start.2
  91.5 5.3 %copy-start.7 = (s32[32,2]{0,1:T(2,128)S(1)}, s32[32,2]{0,1:T(2,128)}, u32[]{:S(2)}) copy-start(s32[32,2]{0,1:T(2,128)} %get-tuple-element.33) | copy-start | bytes 772
  91.5 6.1 %copy-start.9 = (pred[32,2]{0,1:T(4,128)(4,1)S(1)}, pred[32,2]{0,1:T(4,128)(4,1)}, u32[]{:S(2)}) copy-start(pred[32,2]{0,1:T(4,128)(4,1)} %get-tuple-element.32) | copy-start | bytes 196
  91.5 6.2 %copy-start.11 = (pred[32,2]{0,1:T(4,128)(4,1)S(1)}, pred[32,2]{0,1:T(4,128)(4,1)}, u32[]{:S(2)}) copy-start(pred[32,2]{0,1:T(4,128)(4,1)} %get-tuple-element.23) | copy-start | bytes 196
  91.5 7.0 %copy-start.8 = (pred[32,2]{0,1:T(4,128)(4,1)S(1)}, pred[32,2]{0,1:T(4,128)(4,1)}, u32[]{:S(2)}) copy-start(pred[32,2]{0,1:T(4,128)(4,1)} %get-tuple-element.6) | copy-start | bytes 196
  91.5 7.1 %copy-start.10 = (pred[32,2]{0,1:T(4,128)(4,1)S(1)}, pred[32,2]{0,1:T(4,128)(4,1)}, u32[]{:S(2)}) copy-start(pred[32,2]{0,1:T(4,128)(4,1)} %get-tuple-element.18) | copy-start | bytes 196
  91.5 7.8 %copy-start.6 = (s32[32,2]{0,1:T(2,128)S(1)}, s32[32,2]{0,1:T(2,128)}, u32[]{:S(2)}) copy-start(s32[32,2]{0,1:T(2,128)} %get-tuple-element.31) | copy-start | bytes 772
  91.5 34.3 %all-to-all-start.1 = ((bf16[32,64,256]{2,1,0:T(8,128)(2,1)}), bf16[32,64,256]{2,1,0:T(8,128)(2,1)}, u32[]{:S(2)}, u32[]{:S(2)}) async-start(bf16[32,64,256]{2,1,0:T(8,128)(2,1)} %fusion.1), calls=%async_computation.1 | async-start | bytes 2097152 | tf_op jit(solution)/shard_map/all_to_all | solution.py:32
  106.1 0.7 copy-start.5
  144.5 1.6 copy-start
  144.5 2.2 %copy-start.1 = (f32[32,256,64]{1,2,0:T(8,128)S(1)}, f32[32,256,64]{1,2,0:T(8,128)}, u32[]{:S(2)}) copy-start(f32[32,256,64]{1,2,0:T(8,128)} %fusion.4) | copy-start | bytes 6291460
where the time goes:
time: 184 us; the launch traced here: 183 us
  blocking collectives  89.2 us (48%)
  waiting for transfers between devices  40.2 us (22%)
  matrix products  16.8 us (9%)
  starting transfers between devices  14.7 us (8%)
  local copies, waits for them, and re-layouts  12.6 us (7%)
  other arithmetic  9.61 us (5%)
    all_gather x3, blocking collectives, on_device(): gathered.append(lax.all_gather(solved[None], 'row', axis=0, tiled=True))  55.2 us
    all_to_all x2, waiting for transfers between devices, on_device(): lax.all_to_all(partial.astype(jnp.bfloat16), 'col', split_axis=0, concat_...  40.2 us
    all_to_all x1, blocking collectives, on_device(): lax.all_to_all(partial.astype(jnp.bfloat16), 'col', split_axis=0, concat_...  34 us
    dot_general x6, matrix products, level_terms(): jnp.einsum('qik,qkn->qin', blocks, picked, preferred_element_type=jnp.flo...  15.3 us
    all_to_all x2, starting transfers between devices, on_device(): lax.all_to_all(partial.astype(jnp.bfloat16), 'col', split_axis=0, concat_...  14.7 us
    gather x6, local copies, waits for them, and re-layouts, level_terms(): picked = jnp.take(gathered, clipped, axis=0)  4.08 us
  transfers between devices with their start and end apart: 2, of which 2 were waited for; matrix products, arithmetic and copies ran while one was open for 10% of the time, Pallas kernels for 0%

commit v1 on v0

--- a/solution.py
+++ b/solution.py
@@ -42,7 +42,12 @@
         results.append(solution)
         if section + 1 < levels:
             solved = solution.astype(jnp.bfloat16)
-            gathered.append(lax.all_gather(solved[None], "row", axis=0, tiled=True))
+            gathered.append(
+                jnp.concatenate(
+                    lax.all_to_all(jnp.stack([solved[None]] * lax.axis_size("row")), "row", 0, 0),
+                    axis=0,
+                )
+            )
     return jnp.stack(results)[:, None, None]
 
 

time: 184 us -> 198 us (1.076)
  the two profiles are of different devices: /device:TPU:8 before, /device:TPU:1 now
where the time goes in v1:
time: 198 us; the launch traced here: 196 us
  blocking collectives  72.2 us (36%)
  waiting for transfers between devices  61.6 us (31%)
  starting transfers between devices  23.4 us (12%)
  matrix products  17.9 us (9%)
  local copies, waits for them, and re-layouts  13.5 us (7%)
  other arithmetic  7.53 us (4%)
    all_to_all x2, blocking collectives, on_device(): lax.all_to_all(partial.astype(jnp.bfloat16), 'col', split_axis=0, concat_...  72.2 us
    all_to_all x3, waiting for transfers between devices, on_device(): lax.all_to_all(jnp.stack([solved[None]] * lax.axis_size('row')), 'row', 0...  38.7 us
    all_to_all x1, waiting for transfers between devices, on_device(): lax.all_to_all(partial.astype(jnp.bfloat16), 'col', split_axis=0, concat_...  22.9 us
    all_to_all x3, starting transfers between devices, on_device(): lax.all_to_all(jnp.stack([solved[None]] * lax.axis_size('row')), 'row', 0...  18.2 us
    dot_general x6, matrix products, level_terms(): jnp.einsum('qik,qkn->qin', blocks, picked, preferred_element_type=jnp.flo...  14.1 us
    gather x6, local copies, waits for them, and re-layouts, level_terms(): picked = jnp.take(gathered, clipped, axis=0)  5.43 us
    all_to_all x1, starting transfers between devices, on_device(): lax.all_to_all(partial.astype(jnp.bfloat16), 'col', split_axis=0, concat_...  5.25 us
  transfers between devices with their start and end apart: 4, of which 4 were waited for; matrix products, arithmetic and copies ran while one was open for 9% of the time, Pallas kernels for 0%

profile of v1, /device:TPU:1, one launch (start us, length us, event | category | flops | bytes accessed | tf_op | source)
XLA Modules:
  0.0 196.5 jit_solution(6789165908850378322)
XLA Ops:
  0.0 0.9 fusion.40
  0.9 0.9 stack.25
  1.8 10.2 %all-to-all-start = ((bf16[16,1,64,256]{3,2,1,0:T(8,128)(2,1)}), bf16[16,1,64,256]{3,2,1,0:T(8,128)(2,1)S(1)}, u32[]{:S(2)}, u32[]{:S(2)}) async-start(bf16[16,1,64,256]{3,2,1,0:T(8,128)(2,1)} %stack.25), calls=%async_computation | async-start | bytes 1048576 | tf_op jit(solution)/shard_map/all_to_all | solution.py:47
  12.0 0.8 compare_and_fusion.1
  12.8 0.1 copy.26
  12.9 0.1 reshape.167
  13.0 0.1 copy.25
  13.1 0.8 compare_bitcast_fusion.1
  13.9 0.1 copy.24
  14.0 15.4 %all-to-all-done = bf16[16,1,64,256]{3,2,1,0:T(8,128)(2,1)S(1)} async-done(((bf16[16,1,64,256]{3,2,1,0:T(8,128)(2,1)}), bf16[16,1,64,256]{3,2,1,0:T(8,128)(2,1)S(1)}, u32[]{:S(2)}, u32[]{:S(2)}) %all-to-all-start) | async-done | bytes 524320 | tf_op jit(solution)/shard_map/all_to_all | solution.py:47
  29.4 0.7 gather_fusion
  30.1 0.3 select_select_fusion.5
  30.4 1.5 fusion
  31.9 39.3 %all_to_all.30 = bf16[32,64,256]{2,1,0:T(8,128)(2,1)S(1)} all-to-all(bf16[32,64,256]{2,1,0:T(8,128)(2,1)S(1)} %fusion), channel_id=1, replica_groups=mesh['row'=16,'col'=32] {'col'}, dimensions={0} | all-to-all | bytes 2097152 | tf_op jit(solution)/shard_map/all_to_all | solution.py:32
  71.2 0.2 convert_reduce_fusion.2
  71.3 1.0 bitcast_convert_fusion.1
  72.3 0.9 stack.27
  73.2 4.0 %all-to-all-start.2 = ((bf16[16,1,64,256]{3,2,1,0:T(8,128)(2,1)}), bf16[16,1,64,256]{3,2,1,0:T(8,128)(2,1)S(1)}, u32[]{:S(2)}, u32[]{:S(2)}) async-start(bf16[16,1,64,256]{3,2,1,0:T(8,128)(2,1)} %stack.27), calls=%async_computation.2 | async-start | bytes 1048576 | tf_op jit(solution)/shard_map/all_to_all | solution.py:47
  77.2 0.1 reshape.175
  77.3 0.1 copy.31
  77.4 0.1 copy.30
  77.6 0.1 reshape.171
  77.7 0.1 copy.28
  77.8 0.1 copy.27
  78.0 0.7 gather_fusion.1
  78.6 0.3 select_select_fusion.4
  79.0 2.8 %fusion.9 = f32[32,256,64]{1,2,0:T(8,128)} fusion(bf16[32,128,256]{2,1,0:T(8,128)(2,1)S(1)} %bitcast.160, bf16[6,1,1,32,64,128]{5,4,3,2,1,0:T(8,128)(2,1)} %param.8), kind=kOutput, calls=%fused_computation.28 | convolution fusion | flops 134217728 | bytes 4718592 | tf_op jit(solution)/shard_map/qik,qkn->qin/dot_general | solution.py:13
  81.8 12.6 %all-to-all-done.2 = bf16[16,1,64,256]{3,2,1,0:T(8,128)(2,1)S(1)} async-done(((bf16[16,1,64,256]{3,2,1,0:T(8,128)(2,1)}), bf16[16,1,64,256]{3,2,1,0:T(8,128)(2,1)S(1)}, u32[]{:S(2)}, u32[]{:S(2)}) %all-to-all-start.2) | async-done | bytes 524320 | tf_op jit(solution)/shard_map/all_to_all | solution.py:47
  94.5 0.7 gather_fusion.2
  95.1 0.3 select_select_fusion.3
  95.5 1.2 copy-done.2
  96.7 2.6 %fusion.1 = bf16[32,64,256]{2,1,0:T(8,128)(2,1)} fusion(f32[32,256,64]{1,2,0:T(8,128)S(1)} %copy-done.2, bf16[32,128,256]{2,1,0:T(8,128)(2,1)S(1)} %bitcast.164, bf16[6,1,1,32,64,128]{5,4,3,2,1,0:T(8,128)(2,1)} %param.8), kind=kOutput, calls=%fused_computation.19 | convolution fusion | flops 135266304 | bytes 5767168 | tf_op jit(solution)/shard_map/qik,qkn->qin/dot_general | solution.py:13
  99.3 5.2 %all-to-all-start.3 = ((bf16[32,64,256]{2,1,0:T(8,128)(2,1)}), bf16[32,64,256]{2,1,0:T(8,128)(2,1)}, u32[]{:S(2)}, u32[]{:S(2)}) async-start(bf16[32,64,256]{2,1,0:T(8,128)(2,1)} %fusion.1), calls=%async_computation.3 | async-start | bytes 2097152 | tf_op jit(solution)/shard_map/all_to_all | solution.py:32
  104.5 0.1 copy.41
  104.6 0.1 reshape.187
  104.7 0.1 copy.40
  104.8 0.1 copy.39
  105.0 0.1 reshape.183
  105.1 0.1 copy.37
  105.2 0.1 copy.36
  105.4 0.1 reshape.179
  105.5 0.1 copy.34
  105.7 0.1 copy.33
  105.8 2.0 %gather_fusion.3 = bf16[64,64,256]{2,1,0:T(8,128)(2,1)} fusion(bf16[16,64,256]{2,1,0:T(8,128)(2,1)S(1)} %bitcast.149, s32[1024]{0:T(1024)S(1)} %pad_clamp_fusion.2), kind=kCustom, calls=%fused_computation.3.clone | custom fusion | bytes 4194560 | tf_op jit(solution)/shard_map/jit(_take)/gather | solution.py:9
  107.8 1.9 select_select_fusion.2
  109.7 22.9 %all-to-all-done.3 = bf16[32,64,256]{2,1,0:T(8,128)(2,1)} async-done(((bf16[32,64,256]{2,1,0:T(8,128)(2,1)}), bf16[32,64,256]{2,1,0:T(8,128)(2,1)}, u32[]{:S(2)}, u32[]{:S(2)}) %all-to-all-start.3) | async-done | bytes 1048608 | tf_op jit(solution)/shard_map/all_to_all | solution.py:32
  132.6 1.4 convert_reduce_fusion.1
  134.0 1.0 bitcast_convert_fusion
  135.0 0.9 stack.29
  135.8 4.0 %all-to-all-start.4 = ((bf16[16,1,64,256]{3,2,1,0:T(8,128)(2,1)}), bf16[16,1,64,256]{3,2,1,0:T(8,128)(2,1)S(1)}, u32[]{:S(2)}, u32[]{:S(2)}) async-start(bf16[16,1,64,256]{3,2,1,0:T(8,128)(2,1)} %stack.29), calls=%async_computation.4 | async-start | bytes 1048576 | tf_op jit(solution)/shard_map/all_to_all | solution.py:47
  139.8 2.8 %fusion.6 = f32[32,256,64]{1,2,0:T(8,128)} fusion(bf16[32,128,256]{2,1,0:T(8,128)(2,1)S(1)} %bitcast.154, bf16[6,1,1,32,64,128]{5,4,3,2,1,0:T(8,128)(2,1)} %param.8), kind=kOutput, calls=%fused_computation.25 | convolution fusion | flops 134217728 | bytes 4718592 | tf_op jit(solution)/shard_map/qik,qkn->qin/dot_general | solution.py:13
  142.6 0.7 gather_fusion.4
  143.3 0.3 select_select_fusion.1
  143.6 2.8 %fusion.4 = f32[32,256,64]{1,2,0:T(8,128)} fusion(bf16[32,128,256]{2,1,0:T(8,128)(2,1)S(1)} %bitcast.162, bf16[6,1,1,32,64,128]{5,4,3,2,1,0:T(8,128)(2,1)} %param.8), kind=kOutput, calls=%fused_computation.23 | convolution fusion | flops 134217728 | bytes 4718592 | tf_op jit(solution)/shard_map/qik,qkn->qin/dot_general | solution.py:13
  146.4 10.7 %all-to-all-done.4 = bf16[16,1,64,256]{3,2,1,0:T(8,128)(2,1)S(1)} async-done(((bf16[16,1,64,256]{3,2,1,0:T(8,128)(2,1)}), bf16[16,1,64,256]{3,2,1,0:T(8,128)(2,1)S(1)}, u32[]{:S(2)}, u32[]{:S(2)}) %all-to-all-start.4) | async-done | bytes 524320 | tf_op jit(solution)/shard_map/all_to_all | solution.py:47
  157.1 0.7 gather_fusion.5
  157.8 0.3 select_select_fusion
  158.2 1.2 copy-done
  159.4 0.6 copy-done.1
  160.0 1.6 fusion.2
  161.7 33.0 %all_to_all.31 = bf16[32,64,256]{2,1,0:T(8,128)(2,1)S(1)} all-to-all(bf16[32,64,256]{2,1,0:T(8,128)(2,1)S(1)} %fusion.2), channel_id=1, replica_groups=mesh['row'=16,'col'=32] {'col'}, dimensions={0} | all-to-all | bytes 2097152 | tf_op jit(solution)/shard_map/all_to_all | solution.py:32
  194.6 0.2 convert_reduce_fusion
  194.8 1.0 convolution_bitcast_fusion
  195.8 0.7 maximum_bitcast_fusion
  (15 shorter events, 0.4 us)
Async XLA Ops:
  1.8 27.6 %all-to-all-start = ((bf16[16,1,64,256]{3,2,1,0:T(8,128)(2,1)}), bf16[16,1,64,256]{3,2,1,0:T(8,128)(2,1)S(1)}, u32[]{:S(2)}, u32[]{:S(2)}) async-start(bf16[16,1,64,256]{3,2,1,0:T(8,128)(2,1)} %stack.25), calls=%async_computation | async-start | bytes 1048576 | tf_op jit(solution)/shard_map/all_to_all | solution.py:47
  31.9 39.4 %copy-start.3 = (f32[4,1,1,64,64]{4,3,2,1,0:T(8,128)S(1)}, f32[4,1,1,64,64]{4,3,2,1,0:T(8,128)}, u32[]{:S(2)}) copy-start(f32[4,1,1,64,64]{4,3,2,1,0:T(8,128)} %param.7) | copy-start | bytes 196612
  73.2 21.3 %all-to-all-start.2 = ((bf16[16,1,64,256]{3,2,1,0:T(8,128)(2,1)}), bf16[16,1,64,256]{3,2,1,0:T(8,128)(2,1)S(1)}, u32[]{:S(2)}, u32[]{:S(2)}) async-start(bf16[16,1,64,256]{3,2,1,0:T(8,128)(2,1)} %stack.27), calls=%async_computation.2 | async-start | bytes 1048576 | tf_op jit(solution)/shard_map/all_to_all | solution.py:47
  95.1 1.6 copy-start.2
  99.3 33.3 %all-to-all-start.3 = ((bf16[32,64,256]{2,1,0:T(8,128)(2,1)}), bf16[32,64,256]{2,1,0:T(8,128)(2,1)}, u32[]{:S(2)}, u32[]{:S(2)}) async-start(bf16[32,64,256]{2,1,0:T(8,128)(2,1)} %fusion.1), calls=%async_computation.3 | async-start | bytes 2097152 | tf_op jit(solution)/shard_map/all_to_all | solution.py:32
  135.8 21.3 %all-to-all-start.4 = ((bf16[16,1,64,256]{3,2,1,0:T(8,128)(2,1)}), bf16[16,1,64,256]{3,2,1,0:T(8,128)(2,1)S(1)}, u32[]{:S(2)}, u32[]{:S(2)}) async-start(bf16[16,1,64,256]{3,2,1,0:T(8,128)(2,1)} %stack.29), calls=%async_computation.4 | async-start | bytes 1048576 | tf_op jit(solution)/shard_map/all_to_all | solution.py:47
  157.8 1.6 copy-start
  157.8 2.2 %copy-start.1 = (f32[32,256,64]{1,2,0:T(8,128)S(1)}, f32[32,256,64]{1,2,0:T(8,128)}, u32[]{:S(2)}) copy-start(f32[32,256,64]{1,2,0:T(8,128)} %fusion.4) | copy-start | bytes 6291460
